TPU v7x, 128 devices: a whole 4x4x4 slice. The times are simulated.
128 devices in a mesh: row: 8 (over y, core), col: 16 (over z, x).
Axes of the slice: x: 4, y: 4, z: 4, core: 2. Of those that a mesh axis runs over, the one named last changes fastest.
Arguments:
- dealing: int32 [8, 16], P('row'), may hold values from 0 to 15, each once within a row
- residual: bfloat16 [8192, 3072], P('row', 'col'), may hold values from -6 to 6
- queries: bfloat16 [8192, 3072], P('row', 'col'), may hold values from -6 to 6
- draft_keys: bfloat16 [8192, 3072], P('row', 'col'), may hold values from -6 to 6
- draft_values: bfloat16 [8192, 3072], P('row', 'col'), may hold values from -6 to 6
- cache_keys: bfloat16 [128, 1536, 3072], P(('row', 'col')), may hold values from -6 to 6
- cache_values: bfloat16 [128, 1536, 3072], P(('row', 'col')), may hold values from -6 to 6
- cache_lengths: int32 [128], P(('row', 'col')), may hold values from 97 to 1536, as said below
- parents: int32 [128, 64], P(('row', 'col')), may hold values from -1 to 62, as said below
- draft_counts: int32 [128], P(('row', 'col')), may hold values from 32 to 64, as said below
- accepted: int32 [128, 8], P(('row', 'col')), may hold values from -1 to 28, as said below
- out_weight: bfloat16 [3072, 3072], P('row', 'col'), may hold values from -0.109375 to 0.109375
- norm_gain: bfloat16 [3072], P('col'), may hold values from 0.099609375 to 1.8984375
- gate_weight: bfloat16 [3072, 8192], P('row', 'col'), may hold values from -0.109375 to 0.109375
- up_weight: bfloat16 [3072, 8192], P('row', 'col'), may hold values from -0.109375 to 0.109375
- down_weight: bfloat16 [8192, 3072], P('col', 'row'), may hold values from -0.09375 to 0.09375
Outputs:
- layer_out: bfloat16 [8192, 3072], P('row', 'col')
- new_keys: bfloat16 [128, 8, 3072], P(('row', 'col'))
- new_values: bfloat16 [128, 8, 3072], P(('row', 'col'))
Inputs may be any that keep to these rules, and one draw needn't show every extreme that they name: Each row of dealing names every index along col once. `cache_lengths`: the largest is 1536 in every draw. parents[s, 0] = -1, and for i >= 1, i - 4 <= parents[s, i] < i. `draft_counts`: the largest is 64 in every draw. `accepted`: each row lists draft tokens from the root 0 downward, each the child under parents of the one before and below the slot's draft count, then -1; some row fills all 8 entries, and the largest entry is 28 in every draw.
All inputs are finite; a program needn't handle non-finite values.
Results may differ from a plain program's by a relative error of at most 0.017.
Values may be sent and summed in bfloat16 or wider, within the bound.
A program may use at most 128 MiB of HBM per device.

v0:
```python
import math
import jax
import jax.numpy as jnp
from jax import lax
from jax.sharding import PartitionSpec as P

D = 3072
HEADS = 32
HEAD_DIM = 96


def ancestry(parent_row):
    count_all = parent_row.shape[0]
    token_index = jnp.arange(count_all, dtype=jnp.int32)
    linked = jnp.logical_or(
        parent_row[:, None] == token_index[None, :], token_index[:, None] == token_index[None, :]
    )
    ancestors = linked.astype(jnp.float32)
    for sweep in range(max(1, (count_all - 1).bit_length())):
        ancestors = jnp.minimum(jnp.dot(ancestors, ancestors, precision=lax.Precision.HIGHEST), 1.0)
    return ancestors


def rotate(value_rows, position):
    row_count = value_rows.shape[0]
    half_dim = HEAD_DIM // 2
    shaped = value_rows.astype(jnp.float32).reshape(row_count, HEADS, HEAD_DIM)
    frequency = jnp.power(10000.0, -jnp.arange(half_dim, dtype=jnp.float32) * (2.0 / HEAD_DIM))
    angles = position[:, None] * frequency[None, :]
    cosine = jnp.cos(angles)[:, None, :]
    sine_part = jnp.sin(angles)[:, None, :]
    front_half = shaped[..., :half_dim]
    back_half = shaped[..., half_dim:]
    turned = jnp.concatenate(
        [front_half * cosine - back_half * sine_part, back_half * cosine + front_half * sine_part],
        axis=-1,
    )
    return turned.reshape(row_count, HEADS * HEAD_DIM).astype(jnp.bfloat16)


def fold_block(state_now, q_heads, key_block, value_block, allowed):
    running_max, row_totals, accumulator = state_now
    score_scale = 1.0 / math.sqrt(HEAD_DIM)
    key_heads = key_block.reshape(key_block.shape[0], HEADS, HEAD_DIM)
    value_heads = value_block.reshape(value_block.shape[0], HEADS, HEAD_DIM)
    scores = (
        jnp.einsum("qhd,khd->hqk", q_heads, key_heads, preferred_element_type=jnp.float32)
        * score_scale
    )
    scores = jnp.where(allowed[None], scores, -jnp.inf)
    new_max = jnp.maximum(running_max, jnp.max(scores, axis=2))
    rescale = jnp.exp(running_max - new_max)
    weights = jnp.exp(scores - new_max[:, :, None])
    row_totals = row_totals * rescale + jnp.sum(weights, axis=2)
    mixed_rows = jnp.einsum(
        "hqk,khd->qhd",
        weights.astype(jnp.bfloat16),
        value_heads,
        preferred_element_type=jnp.float32,
    )
    accumulator = accumulator * rescale.T[:, :, None] + mixed_rows
    return (new_max, row_totals, accumulator)


def verify_slot(
    query_rows, key_rows, value_rows, cache_k, cache_v, length, parent_row, live_count, path_row
):
    draft_rows = query_rows.shape[0]
    width = query_rows.shape[1]
    ancestors = ancestry(parent_row)
    tree_depth = jnp.sum(ancestors, axis=1) - 1.0
    position = length.astype(jnp.float32) + tree_depth
    q_rot = rotate(query_rows, position)
    k_rot = rotate(key_rows, position)
    q_heads = q_rot.reshape(draft_rows, HEADS, HEAD_DIM)
    cache_rows = cache_k.shape[0]
    block_rows = min(512, cache_rows)

    def cache_step(block_step, state_now):
        block_start = block_step * block_rows
        key_block = lax.dynamic_slice_in_dim(cache_k, block_start, block_rows, 0)
        value_block = lax.dynamic_slice_in_dim(cache_v, block_start, block_rows, 0)
        live_keys = block_start + jnp.arange(block_rows, dtype=jnp.int32) < length
        allowed = jnp.broadcast_to(live_keys[None, :], (draft_rows, block_rows))
        return fold_block(state_now, q_heads, key_block, value_block, allowed)

    initial = (
        jnp.full((HEADS, draft_rows), -jnp.inf, jnp.float32),
        jnp.zeros((HEADS, draft_rows), jnp.float32),
        jnp.zeros((draft_rows, HEADS, HEAD_DIM), jnp.float32),
    )
    block_total = cache_rows // block_rows
    state_now = lax.fori_loop(0, block_total, cache_step, initial)
    token_index = jnp.arange(draft_rows, dtype=jnp.int32)
    allowed = jnp.logical_and(ancestors > 0.5, token_index[None, :] < live_count)
    running_max, row_totals, accumulator = fold_block(
        state_now, q_heads, k_rot, value_rows, allowed
    )
    attended = (
        (accumulator / row_totals.T[:, :, None]).reshape(draft_rows, width).astype(jnp.bfloat16)
    )
    selector = (path_row[:, None] == token_index[None, :]).astype(jnp.bfloat16)
    new_keys = jnp.dot(selector, k_rot, preferred_element_type=jnp.float32).astype(jnp.bfloat16)
    new_values = jnp.dot(selector, value_rows, preferred_element_type=jnp.float32).astype(
        jnp.bfloat16
    )
    return (attended, new_keys, new_values)


def body(
    dealing,
    residual,
    queries,
    draft_keys,
    draft_values,
    cache_keys,
    cache_values,
    cache_lengths,
    parents,
    draft_counts,
    accepted,
    out_weight,
    norm_gain,
    gate_weight,
    up_weight,
    down_weight,
):
    columns = lax.axis_size("col")
    dealt_order = dealing[0]
    rows_here = residual.shape[0]
    draft_rows = rows_here // columns

    def to_slots(block_rows):
        shaped = block_rows.reshape(columns, draft_rows, block_rows.shape[1])
        return jnp.take(shaped, dealt_order, axis=0).reshape(rows_here, block_rows.shape[1])

    mine_q, mine_k, mine_v = (
        lax.all_to_all(to_slots(queries), "col", split_axis=0, concat_axis=1, tiled=True),
        lax.all_to_all(to_slots(draft_keys), "col", split_axis=0, concat_axis=1, tiled=True),
        lax.all_to_all(to_slots(draft_values), "col", split_axis=0, concat_axis=1, tiled=True),
    )
    attended, new_keys, new_values = verify_slot(
        mine_q,
        mine_k,
        mine_v,
        cache_keys[0],
        cache_values[0],
        cache_lengths[0],
        parents[0],
        draft_counts[0],
        accepted[0],
    )
    weight_cols = lax.all_gather(out_weight, "row", axis=0, tiled=True)
    projected = jnp.dot(
        lax.all_gather(attended, "col", axis=0, tiled=True),
        weight_cols,
        preferred_element_type=jnp.float32,
    )
    inverse = jnp.argsort(dealt_order)
    projected = jnp.take(
        projected.reshape(columns, draft_rows, projected.shape[1]), inverse, axis=0
    ).reshape(rows_here, projected.shape[1])
    stream_full = residual.astype(jnp.float32) + projected
    stream = stream_full.astype(jnp.bfloat16)
    stream_wide = lax.optimization_barrier(stream).astype(jnp.float32)
    local_sums = jnp.sum(stream_wide * stream_wide, axis=1)
    row_totals = lax.psum(local_sums, "col")
    factor = lax.rsqrt(row_totals / D + 1e-05)[:, None]
    normed = (stream_wide * factor * norm_gain.astype(jnp.float32)[None, :]).astype(jnp.bfloat16)
    gathered = lax.all_gather(normed, "col", axis=1, tiled=True)
    gate_next = jnp.dot(
        gathered,
        lax.all_gather(gate_weight, "row", axis=0, tiled=True),
        preferred_element_type=jnp.float32,
    )
    up_next = jnp.dot(
        gathered,
        lax.all_gather(up_weight, "row", axis=0, tiled=True),
        preferred_element_type=jnp.float32,
    )
    hidden = (jax.nn.silu(gate_next) * up_next).astype(jnp.bfloat16)
    partial_terms = jnp.dot(
        hidden,
        lax.all_gather(down_weight, "row", axis=1, tiled=True),
        preferred_element_type=jnp.float32,
    )
    summed = lax.psum_scatter(
        partial_terms.astype(jnp.bfloat16), "col", scatter_dimension=1, tiled=True
    ).astype(jnp.float32)
    layer_out = (stream_wide + summed).astype(jnp.bfloat16)
    return (layer_out, new_keys[None], new_values[None])


def solution(mesh):
    placed = (
        P("row", None),
        P("row", "col"),
        P("row", "col"),
        P("row", "col"),
        P("row", "col"),
        P(("row", "col"), None, None),
        P(("row", "col"), None, None),
        P(("row", "col")),
        P(("row", "col"), None),
        P(("row", "col")),
        P(("row", "col"), None),
        P("row", "col"),
        P("col"),
        P("row", "col"),
        P("row", "col"),
        P("col", "row"),
    )
    return jax.shard_map(
        body,
        mesh=mesh,
        in_specs=placed,
        out_specs=(P("row", "col"), P(("row", "col"), None, None), P(("row", "col"), None, None)),
        check_vma=False,
    )
```

profile of v0, /device:TPU:0, one launch (start us, length us, event | category | flops | bytes accessed | tf_op | source)
XLA Modules:
  0.0 458.0 jit_solution(15680085825392630706)
XLA Ops:
  14.3 8.0 %all-to-all-start.1 = ((bf16[16,64,192]{2,1,0:T(8,128)(2,1)}), bf16[16,64,192]{2,1,0:T(8,128)(2,1)S(1)}, u32[]{:S(2)}, u32[]{:S(2)}) async-start(bf16[16,64,192]{2,1,0:T(8,128)(2,1)} %get-tuple-element.212), calls=%async_computation.1 | async-start | bytes 1048576 | tf_op jit(solution)/shard_map/all_to_all | solution.py:139
  25.6 12.8 %copy.22 = bf16[1,1536,3072]{1,2,0:T(8,128)(2,1)} copy(bf16[1,1536,3072]{2,1,0:T(8,128)(2,1)} %param.25) | data formatting | bytes 18874368 | tf_op args[5]
  38.4 12.6 %copy.27 = bf16[1,1536,3072]{1,2,0:T(8,128)(2,1)} copy(bf16[1,1536,3072]{2,1,0:T(8,128)(2,1)} %param.26) | data formatting | bytes 18874368 | tf_op args[6]
  51.2 7.4 %all-to-all-start = ((bf16[16,64,192]{2,1,0:T(8,128)(2,1)}), bf16[16,64,192]{2,1,0:T(8,128)(2,1)}, u32[]{:S(2)}, u32[]{:S(2)}) async-start(bf16[16,64,192]{2,1,0:T(8,128)(2,1)} %get-tuple-element.213), calls=%async_computation | async-start | bytes 1048576 | tf_op jit(solution)/shard_map/all_to_all | solution.py:138
  60.0 9.6 %all-to-all-done = bf16[16,64,192]{2,1,0:T(8,128)(2,1)} async-done(((bf16[16,64,192]{2,1,0:T(8,128)(2,1)}), bf16[16,64,192]{2,1,0:T(8,128)(2,1)}, u32[]{:S(2)}, u32[]{:S(2)}) %all-to-all-start) | async-done | bytes 393248 | tf_op jit(solution)/shard_map/all_to_all | solution.py:138
  69.5 4.2 all-to-all-start.2
  75.1 1.6 copy.24
  81.0 1.6 maximum_convert_fusion
  82.6 40.6 %while.18 = (s32[]{:T(128)}, f32[32,64]{1,0:T(8,128)S(1)}, f32[32,64]{1,0:T(8,128)S(1)}, f32[64,32,96]{2,0,1:T(8,128)}, s32[]{:T(128)}, /*index=5*/bf16[1536,307...) while((s32[]{:T(128)}, f32[32,64]{1,0:T(8,128)S(1)}, ...), condition=%wide.region_5.7_spmd.clone, body=%wide.region_2.6_spmd.clone.sunk | while | flops 414790656 | bytes 51906808 | solution.py:93
  83.3 3.3 constant_dynamic-slice_fusion.3
  86.7 2.8 bitcast_reduce_fusion.2
  89.5 3.4 fusion.84
  92.9 2.6 fusion.86
  96.2 3.3 constant_dynamic-slice_fusion.3
  99.5 2.8 bitcast_reduce_fusion.2
  102.3 3.4 fusion.84
  105.8 3.6 fusion.86
  110.0 3.3 constant_dynamic-slice_fusion.3
  113.4 2.8 bitcast_reduce_fusion.2
  116.2 3.4 fusion.84
  119.6 3.6 fusion.86
  124.9 1.6 fusion.44
  132.4 60.7 %all-gather.7.cloned.1.call-done = bf16[1024,3072]{1,0:T(8,128)(2,1)} async-done(((bf16[64,3072]{1,0:T(8,128)(2,1)}), bf16[1024,3072]{1,0:T(8,128)(2,1)}) %all-gather.7.cloned.1.call-update) | async-done | bytes 6291472 | tf_op jit(solution)/shard_map/all_gather | solution.py:155
  193.1 4.9 %fusion.45 = f32[1024,192]{1,0:T(8,128)S(1)} fusion(bf16[1024,3072]{1,0:T(8,128)(2,1)} %all-gather.7.cloned.1.call-done, bf16[3072,192]{0,1:T(8,128)(2,1)} %all-gather.9.cloned.1.call-done), kind=kOutput, calls=%fused_computation.98 | convolution fusion | flops 1207959552 | bytes 8257536 | tf_op jit(solution)/shard_map/dot_general | solution.py:154
  199.3 38.4 %psum.7 = f32[1024]{0:T(1024)S(1)} all-reduce(f32[1024]{0:T(1024)S(1)} %fusion.27), channel_id=1, replica_groups=mesh['row'=8,'col'=16] {'col'}, use_global_device_ids=true, to_apply=%region_9.11 | all-reduce | flops 1024 | bytes 8192 | tf_op jit(solution)/shard_map/psum | solution.py:167
  239.8 56.6 %all-gather.11.cloned.1.call-done = bf16[1024,3072]{0,1:T(8,128)(2,1)} async-done(((bf16[1024,192]{0,1:T(8,128)(2,1)}), bf16[1024,3072]{0,1:T(8,128)(2,1)}) %all-gather.11.cloned.1.call-update) | async-done | bytes 6291472 | tf_op jit(solution)/shard_map/all_gather | solution.py:170
  296.4 6.5 %fusion.46 = f32[1024,512]{1,0:T(8,128)S(1)} fusion(bf16[1024,3072]{0,1:T(8,128)(2,1)} %all-gather.11.cloned.1.call-done, bf16[3072,512]{1,0:T(8,128)(2,1)} %all-gather.13.cloned.1.call-done), kind=kOutput, calls=%fused_computation.99 | convolution fusion | flops 3221225472 | bytes 11534336 | tf_op jit(solution)/shard_map/dot_general | solution.py:171
  302.9 22.3 %all-gather.17.cloned.1.call-done = bf16[512,3072]{1,0:T(8,128)(2,1)} async-done(((bf16[512,384]{1,0:T(8,128)(2,1)}), bf16[512,3072]{1,0:T(8,128)(2,1)}) %all-gather.17.cloned.1.call-update) | async-done | bytes 3145744 | tf_op jit(solution)/shard_map/all_gather | solution.py:184
  325.2 29.4 %all-gather.15.cloned.1.call-done = bf16[3072,512]{1,0:T(8,128)(2,1)} async-done(((bf16[384,512]{1,0:T(8,128)(2,1)}), bf16[3072,512]{1,0:T(8,128)(2,1)}) %all-gather.15.cloned.1.call-update) | async-done | bytes 3145744 | tf_op jit(solution)/shard_map/all_gather | solution.py:178
  354.6 12.8 %convolution_convert_fusion = bf16[1024,3072]{0,1:T(8,128)(2,1)} fusion(bf16[512,3072]{1,0:T(8,128)(2,1)} %all-gather.17.cloned.1.call-done, f32[1024,512]{1,0:T(8,128)S(1)} %fusion.46, bf16[1024,3072]{0,1:T(8,128)(2,1)} %all-gather.11.cloned.1.call-done, bf16[3072,512]{1,0:T(8,128)(2,1)} %all-gather.15.cloned.1.call-done), kind=kOutput, calls=%fused_computation.28 | convolution fusion | flops 6448742400 | bytes 20971520 | tf_op jit(solution)/shard_map/dot_general | solution.py:182
  371.8 77.5 %reduce-scatter.2.cloned.1.call-done = bf16[1024,192]{0,1:T(8,128)(2,1)} async-done(((bf16[1024,3072]{0,1:T(8,128)(2,1)}), bf16[1024,192]{0,1:T(8,128)(2,1)}) %reduce-scatter.2.cloned.1.call-update) | async-done | bytes 393232 | tf_op jit(solution)/shard_map/reduce_scatter | solution.py:187
  449.3 1.9 fusion.30
  (118 shorter events, 33.3 us)
Async XLA Ops:
  7.2 5.0 %copy-start.3 = (bf16[1024,192]{0,1:T(8,128)(2,1)S(1)}, bf16[1024,192]{0,1:T(8,128)(2,1)}, u32[]{:S(2)}) copy-start(bf16[1024,192]{0,1:T(8,128)(2,1)} %param.22) | copy-start | bytes 1179652
  11.0 12.1 %copy-start.6 = (s32[1,64]{1,0:T(1,128)S(1)}, s32[1,64]{1,0:T(1,128)}, u32[]{:S(2)}) copy-start(s32[1,64]{1,0:T(1,128)} %param.28) | copy-start | bytes 772
  14.3 36.9 %all-to-all-start.1 = ((bf16[16,64,192]{2,1,0:T(8,128)(2,1)}), bf16[16,64,192]{2,1,0:T(8,128)(2,1)S(1)}, u32[]{:S(2)}, u32[]{:S(2)}) async-start(bf16[16,64,192]{2,1,0:T(8,128)(2,1)} %get-tuple-element.212), calls=%async_computation.1 | async-start | bytes 1048576 | tf_op jit(solution)/shard_map/all_to_all | solution.py:139
  22.3 110.1 %all-gather.9.cloned.1.call-start = ((), (), s32[]{:S(2)}) async-start(), calls=%async_computation.5 | async-start | bytes 1327104 | tf_op jit(solution)/shard_map/all_gather | solution.py:153
  51.2 18.3 %all-to-all-start = ((bf16[16,64,192]{2,1,0:T(8,128)(2,1)}), bf16[16,64,192]{2,1,0:T(8,128)(2,1)}, u32[]{:S(2)}, u32[]{:S(2)}) async-start(bf16[16,64,192]{2,1,0:T(8,128)(2,1)} %get-tuple-element.213), calls=%async_computation | async-start | bytes 1048576 | tf_op jit(solution)/shard_map/all_to_all | solution.py:138
  69.5 53.7 %all-to-all-start.2 = ((bf16[16,64,192]{2,1,0:T(8,128)(2,1)}), bf16[16,64,192]{2,1,0:T(8,128)(2,1)}, u32[]{:S(2)}, u32[]{:S(2)}) async-start(bf16[16,64,192]{2,1,0:T(8,128)(2,1)} %get-tuple-element.211), calls=%async_computation.2 | async-start | bytes 1048576 | tf_op jit(solution)/shard_map/all_to_all | solution.py:140
  73.8 119.4 %all-gather.7.cloned.1.call-start = ((), (), s32[]{:S(2)}) async-start(), calls=%async_computation.4 | async-start | bytes 6684672 | tf_op jit(solution)/shard_map/all_gather | solution.py:155
  83.3 3.3 copy-start.1
  89.5 3.4 copy-start
  96.2 3.3 copy-start.1
  102.3 3.4 copy-start
  110.0 3.3 copy-start.1
  116.2 3.4 copy-start
  123.2 3.6 copy-start.9
  126.8 4.2 copy-start.7
  126.8 5.6 %copy-start.8 = (bf16[192]{0:T(256)(128)(2,1)S(1)}, bf16[192]{0:T(256)(128)(2,1)}, u32[]{:S(2)}) copy-start(bf16[192]{0:T(256)(128)(2,1)} %param.32) | copy-start | bytes 1156
  129.9 109.9 %all-gather.13.cloned.1.call-start = ((), (), s32[]{:S(2)}) async-start(), calls=%async_computation.7 | async-start | bytes 3538944 | tf_op jit(solution)/shard_map/all_gather | solution.py:173
  130.7 165.7 %all-gather.11.cloned.1.call-start = ((), (), s32[]{:S(2)}) async-start(), calls=%async_computation.6 | async-start | bytes 6684672 | tf_op jit(solution)/shard_map/all_gather | solution.py:170
  198.0 1.0 copy-start.4
  238.6 86.7 %all-gather.17.cloned.1.call-start = ((), (), s32[]{:S(2)}) async-start(), calls=%async_computation.9 | async-start | bytes 3538944 | tf_op jit(solution)/shard_map/all_gather | solution.py:184
  239.2 115.5 %all-gather.15.cloned.1.call-start = ((), (), s32[]{:S(2)}) async-start(), calls=%async_computation.8 | async-start | bytes 3538944 | tf_op jit(solution)/shard_map/all_gather | solution.py:178
  239.8 209.5 %reduce-scatter.2.cloned.1.call-start = ((), (), s32[]{:S(2)}) async-start(), calls=%async_computation.10 | async-start | bytes 6684672 | tf_op jit(solution)/shard_map/reduce_scatter | solution.py:187
  367.5 1.0 copy-start.2
  367.5 2.7 copy-start.5
Sparse Core Ops, SparseCore 0:
  24.8 25.2 all-gather.8
  130.1 63.0 all-gather.6
  194.8 27.2 all-gather.12
  238.7 57.6 all-gather.10
  298.0 27.2 all-gather.16
  326.8 27.8 all-gather.14
  367.6 81.6 reduce-scatter.1
where the time goes:
time: 459 us; the launch traced here: 458 us
  waiting for transfers between devices  259 us (56%)
  local copies, waits for them, and re-layouts  51.6 us (11%)
  matrix products  48 us (10%)
  blocking collectives  38.4 us (8%)
  other arithmetic  25 us (5%)
  starting transfers between devices  20.3 us (4%)
  between operations  15.9 us (3%)
    reduce_scatter x1, waiting for transfers between devices, body(): lax.psum_scatter(partial_terms.astype(jnp.bfloat16), 'col', scatter_dimen...  77.5 us
    all_gather x1, waiting for transfers between devices, body(): lax.all_gather(attended, 'col', axis=0, tiled=True)  60.7 us
    all_gather x1, waiting for transfers between devices, body(): gathered = lax.all_gather(normed, 'col', axis=1, tiled=True)  56.6 us
    psum x1, blocking collectives, body(): row_totals = lax.psum(local_sums, 'col')  38.4 us
    all_gather x1, waiting for transfers between devices, body(): lax.all_gather(up_weight, 'row', axis=0, tiled=True)  29.4 us
    unnamed x21, local copies, waits for them, and re-layouts  29 us
    all_gather x1, waiting for transfers between devices, body(): lax.all_gather(down_weight, 'row', axis=1, tiled=True)  22.3 us
    dot_general x1, matrix products, body(): jnp.dot(hidden, lax.all_gather(down_weight, 'row', axis=1, tiled=True), p...  12.8 us
  transfers between devices with their start and end apart: 10, of which 6 were waited for; matrix products, arithmetic and copies ran while one was open for 22% of the time, Pallas kernels for 0%

commit v1 on v0

--- a/solution.py
+++ b/solution.py
@@ -7,6 +7,38 @@
 D = 3072
 HEADS = 32
 HEAD_DIM = 96
+
+
+def supply_all_marks_now(point, axis_k):
+    after = list(point.shape[1:])
+    after[axis_k] *= point.shape[0]
+    return jnp.moveaxis(point, 0, axis_k).reshape(after)
+
+
+def move_counts(matrix, group_axis, out_dim):
+    many = lax.axis_size(group_axis)
+    store = []
+    h = 0
+    while h < many:
+        store.append((h, (h + 1) % many))
+        h += 1
+    slots = []
+    for u, ii in store:
+        slots.append((ii, u))
+    val, current_arr = ([], [])
+    pp = 0
+    while pp < many - 1:
+        if pp % 2 == 0:
+            val.append(lax.ppermute(val[-1] if val else matrix, group_axis, store))
+        else:
+            current_arr.append(
+                lax.ppermute(current_arr[-1] if current_arr else matrix, group_axis, slots)
+            )
+        pp += 1
+    x_new = jnp.stack([*val[::-1], matrix, *current_arr])
+    z_new = lax.axis_index(group_axis) - len(val)
+    x_new = x_new[(jnp.arange(many) - z_new) % many]
+    return supply_all_marks_now(x_new, out_dim)
 
 
 def ancestry(parent_row):
@@ -174,9 +206,7 @@
         preferred_element_type=jnp.float32,
     )
     up_next = jnp.dot(
-        gathered,
-        lax.all_gather(up_weight, "row", axis=0, tiled=True),
-        preferred_element_type=jnp.float32,
+        gathered, move_counts(up_weight, "row", 0), preferred_element_type=jnp.float32
     )
     hidden = (jax.nn.silu(gate_next) * up_next).astype(jnp.bfloat16)
     partial_terms = jnp.dot(

time: 459 us -> 430 us (0.937)
  waiting for transfers between devices: 259 us -> 209 us
  local copies, waits for them, and re-layouts: 51.6 us -> 63.2 us
  starting transfers between devices: 20.3 us -> 29.3 us
    all_gather x1, waiting for transfers between devices: 56.6 us -> 11.8 us  [body(): gathered = lax.all_gather(normed, 'col', axis=1, tiled=True)]
    all_gather x1 -> x0, waiting for transfers between devices: 29.4 us -> none  [body(): lax.all_gather(up_weight, 'row', axis=0, tiled=True)]
    ppermute x0 -> x7, waiting for transfers between devices: none -> 24.7 us  [the longest x4 24.7 us: move_counts(): val.append(lax.ppermute(val[-1] if val else matrix, group_axis, store))]
    ppermute x0 -> x7, starting transfers between devices: none -> 9.03 us  [the longest x3 9 us: move_counts(): lax.ppermute(current_arr[-1] if current_arr else matrix, group_axis, slots)]
    unnamed x21 -> x30, local copies, waits for them, and re-layouts: 29 us -> 35.5 us
  transfers between devices with their start and end apart: 10 -> 16, of which waited for: 6 -> 9; matrix products, arithmetic and copies ran while one was open for 22% -> 26% of each run, Pallas kernels for 0% -> 0%
where the time goes in v1:
time: 430 us; the launch traced here: 429 us
  waiting for transfers between devices  209 us (49%)
  local copies, waits for them, and re-layouts  63.2 us (15%)
  matrix products  48 us (11%)
  blocking collectives  38.4 us (9%)
  starting transfers between devices  29.3 us (7%)
  other arithmetic  25 us (6%)
  between operations  15.9 us (4%)
    reduce_scatter x1, waiting for transfers between devices, body(): lax.psum_scatter(partial_terms.astype(jnp.bfloat16), 'col', scatter_dimen...  77.7 us
    all_gather x1, waiting for transfers between devices, body(): lax.all_gather(attended, 'col', axis=0, tiled=True)  60.7 us
    psum x1, blocking collectives, body(): row_totals = lax.psum(local_sums, 'col')  38.4 us
    unnamed x30, local copies, waits for them, and re-layouts  35.5 us
    ppermute x4, waiting for transfers between devices, move_counts(): val.append(lax.ppermute(val[-1] if val else matrix, group_axis, store))  24.7 us
    all_gather x1, waiting for transfers between devices, body(): lax.all_gather(down_weight, 'row', axis=1, tiled=True)  22.3 us
    dot_general x1, matrix products, body(): jnp.dot(hidden, lax.all_gather(down_weight, 'row', axis=1, tiled=True), p...  12.8 us
    all_gather x1, waiting for transfers between devices, body(): gathered = lax.all_gather(normed, 'col', axis=1, tiled=True)  11.8 us
  transfers between devices with their start and end apart: 16, of which 9 were waited for; matrix products, arithmetic and copies ran while one was open for 26% of the time, Pallas kernels for 0%

profile of v1, /device:TPU:0, one launch (start us, length us, event | category | flops | bytes accessed | tf_op | source)
XLA Modules:
  0.0 428.7 jit_solution(16160741608175756156)
XLA Ops:
  14.3 8.0 %all-to-all-start.1 = ((bf16[16,64,192]{2,1,0:T(8,128)(2,1)}), bf16[16,64,192]{2,1,0:T(8,128)(2,1)S(1)}, u32[]{:S(2)}, u32[]{:S(2)}) async-start(bf16[16,64,192]{2,1,0:T(8,128)(2,1)} %get-tuple-element.212), calls=%async_computation.1 | async-start | bytes 1048576 | tf_op jit(solution)/shard_map/all_to_all | solution.py:171
  25.6 12.7 %copy.22 = bf16[1,1536,3072]{1,2,0:T(8,128)(2,1)} copy(bf16[1,1536,3072]{2,1,0:T(8,128)(2,1)} %param.25) | data formatting | bytes 18874368 | tf_op args[5]
  38.3 12.6 %copy.27 = bf16[1,1536,3072]{1,2,0:T(8,128)(2,1)} copy(bf16[1,1536,3072]{2,1,0:T(8,128)(2,1)} %param.26) | data formatting | bytes 18874368 | tf_op args[6]
  51.1 7.4 %all-to-all-start = ((bf16[16,64,192]{2,1,0:T(8,128)(2,1)}), bf16[16,64,192]{2,1,0:T(8,128)(2,1)}, u32[]{:S(2)}, u32[]{:S(2)}) async-start(bf16[16,64,192]{2,1,0:T(8,128)(2,1)} %get-tuple-element.213), calls=%async_computation | async-start | bytes 1048576 | tf_op jit(solution)/shard_map/all_to_all | solution.py:170
  59.9 9.6 %all-to-all-done = bf16[16,64,192]{2,1,0:T(8,128)(2,1)} async-done(((bf16[16,64,192]{2,1,0:T(8,128)(2,1)}), bf16[16,64,192]{2,1,0:T(8,128)(2,1)}, u32[]{:S(2)}, u32[]{:S(2)}) %all-to-all-start) | async-done | bytes 393248 | tf_op jit(solution)/shard_map/all_to_all | solution.py:170
  69.5 4.2 all-to-all-start.2
  82.6 40.5 %while.18 = (s32[]{:T(128)}, f32[32,64]{1,0:T(8,128)S(1)}, f32[32,64]{1,0:T(8,128)S(1)}, f32[64,32,96]{2,0,1:T(8,128)}, s32[]{:T(128)}, /*index=5*/bf16[1536,307...) while((s32[]{:T(128)}, f32[32,64]{1,0:T(8,128)S(1)}, ...), condition=%wide.region_5.7_spmd.clone, body=%wide.region_2.6_spmd.clone.sunk | while | flops 414790656 | bytes 51906808 | solution.py:125
  83.3 3.3 constant_dynamic-slice_fusion.3
  89.4 3.4 fusion.86
  96.1 3.3 constant_dynamic-slice_fusion.3
  102.3 3.4 fusion.86
  105.7 3.6 fusion.88
  110.0 3.3 constant_dynamic-slice_fusion.3
  113.3 2.8 bitcast_reduce_fusion.2
  116.1 3.4 fusion.86
  119.6 3.6 fusion.88
  132.4 60.7 %all-gather.6.cloned.1.call-done = bf16[1024,3072]{1,0:T(8,128)(2,1)} async-done(((bf16[64,3072]{1,0:T(8,128)(2,1)}), bf16[1024,3072]{1,0:T(8,128)(2,1)}) %all-gather.6.cloned.1.call-update) | async-done | bytes 6291472 | tf_op jit(solution)/shard_map/all_gather | solution.py:187
  193.1 4.9 %fusion.47 = f32[1024,192]{1,0:T(8,128)S(1)} fusion(bf16[1024,3072]{1,0:T(8,128)(2,1)} %all-gather.6.cloned.1.call-done, bf16[3072,192]{0,1:T(8,128)(2,1)} %all-gather.8.cloned.1.call-done), kind=kOutput, calls=%fused_computation.114 | convolution fusion | flops 1207959552 | bytes 8257536 | tf_op jit(solution)/shard_map/dot_general | solution.py:186
  199.2 38.4 %psum.7 = f32[1024]{0:T(1024)S(1)} all-reduce(f32[1024]{0:T(1024)S(1)} %fusion.27), channel_id=1, replica_groups=mesh['row'=8,'col'=16] {'col'}, use_global_device_ids=true, to_apply=%region_9.11 | all-reduce | flops 1024 | bytes 8192 | tf_op jit(solution)/shard_map/psum | solution.py:199
  239.2 8.4 %collective-permute-done = bf16[384,512]{1,0:T(8,128)(2,1)S(1)} collective-permute-done((bf16[384,512]{1,0:T(8,128)(2,1)S(1)}, bf16[384,512]{1,0:T(8,128)(2,1)S(1)}, u32[]{:S(2)}, u32[]{:S(2)}) %collective-permute-start) | collective-permute-done | bytes 393248 | tf_op jit(solution)/shard_map/ppermute | solution.py:32
  247.6 3.0 collective-permute-start.4
  250.5 5.5 %collective-permute-done.1 = bf16[384,512]{1,0:T(8,128)(2,1)S(1)} collective-permute-done((bf16[384,512]{1,0:T(8,128)(2,1)S(1)}, bf16[384,512]{1,0:T(8,128)(2,1)S(1)}, u32[]{:S(2)}, u32[]{:S(2)}) %collective-permute-start.1) | collective-permute-done | bytes 393248 | tf_op jit(solution)/shard_map/ppermute | solution.py:32
  256.0 3.0 collective-permute-start.5
  259.0 5.4 %collective-permute-done.2 = bf16[384,512]{1,0:T(8,128)(2,1)S(1)} collective-permute-done((bf16[384,512]{1,0:T(8,128)(2,1)S(1)}, bf16[384,512]{1,0:T(8,128)(2,1)S(1)}, u32[]{:S(2)}, u32[]{:S(2)}) %collective-permute-start.2) | collective-permute-done | bytes 393248 | tf_op jit(solution)/shard_map/ppermute | solution.py:32
  264.4 3.0 collective-permute-start.6
  267.5 5.5 %collective-permute-done.3 = bf16[384,512]{1,0:T(8,128)(2,1)} collective-permute-done((bf16[384,512]{1,0:T(8,128)(2,1)S(1)}, bf16[384,512]{1,0:T(8,128)(2,1)}, u32[]{:S(2)}, u32[]{:S(2)}) %collective-permute-start.3) | collective-permute-done | bytes 393248 | tf_op jit(solution)/shard_map/ppermute | solution.py:32
  280.2 4.4 %gather_fusion.1 = bf16[8,384,512]{2,1,0:T(8,128)(2,1)} fusion(bf16[8,384,512]{2,1,0:T(8,128)(2,1)} %bitcast_dynamic-update-slice_fusion, s32[1024]{0:T(1024)S(1)} %pad_clamp_fusion), kind=kCustom, calls=%fused_computation.4 | custom fusion | bytes 6291488 | tf_op jit(solution)/shard_map/gather | solution.py:40
  284.6 11.8 %all-gather.10.cloned.1.call-done = bf16[1024,3072]{0,1:T(8,128)(2,1)} async-done(((bf16[1024,192]{0,1:T(8,128)(2,1)}), bf16[1024,3072]{0,1:T(8,128)(2,1)}) %all-gather.10.cloned.1.call-update) | async-done | bytes 6291472 | tf_op jit(solution)/shard_map/all_gather | solution.py:202
  296.3 6.5 %fusion.48 = f32[1024,512]{1,0:T(8,128)S(1)} fusion(bf16[1024,3072]{0,1:T(8,128)(2,1)} %all-gather.10.cloned.1.call-done, bf16[3072,512]{1,0:T(8,128)(2,1)} %all-gather.12.cloned.1.call-done), kind=kOutput, calls=%fused_computation.115 | convolution fusion | flops 3221225472 | bytes 11534336 | tf_op jit(solution)/shard_map/dot_general | solution.py:203
  302.8 22.3 %all-gather.14.cloned.1.call-done = bf16[512,3072]{1,0:T(8,128)(2,1)} async-done(((bf16[512,384]{1,0:T(8,128)(2,1)}), bf16[512,3072]{1,0:T(8,128)(2,1)}) %all-gather.14.cloned.1.call-update) | async-done | bytes 3145744 | tf_op jit(solution)/shard_map/all_gather | solution.py:214
  325.2 12.8 %convolution_convert_fusion = bf16[1024,3072]{0,1:T(8,128)(2,1)} fusion(bf16[512,3072]{1,0:T(8,128)(2,1)} %all-gather.14.cloned.1.call-done, f32[1024,512]{1,0:T(8,128)S(1)} %fusion.48, bf16[1024,3072]{0,1:T(8,128)(2,1)} %all-gather.10.cloned.1.call-done, bf16[3072,512]{1,0:T(8,128)(2,1)} %bitcast.128), kind=kOutput, calls=%fused_computation.29 | convolution fusion | flops 6448742400 | bytes 20971520 | tf_op jit(solution)/shard_map/dot_general | solution.py:212
  342.3 77.7 %reduce-scatter.2.cloned.1.call-done = bf16[1024,192]{0,1:T(8,128)(2,1)} async-done(((bf16[1024,3072]{0,1:T(8,128)(2,1)}), bf16[1024,192]{0,1:T(8,128)(2,1)}) %reduce-scatter.2.cloned.1.call-update) | async-done | bytes 393232 | tf_op jit(solution)/shard_map/reduce_scatter | solution.py:217
  (142 shorter events, 54.9 us)
Async XLA Ops:
  7.2 5.0 %copy-start.3 = (bf16[1024,192]{0,1:T(8,128)(2,1)S(1)}, bf16[1024,192]{0,1:T(8,128)(2,1)}, u32[]{:S(2)}) copy-start(bf16[1024,192]{0,1:T(8,128)(2,1)} %param.22) | copy-start | bytes 1179652
  12.2 10.9 %copy-start.7 = (s32[1,64]{1,0:T(1,128)S(1)}, s32[1,64]{1,0:T(1,128)}, u32[]{:S(2)}) copy-start(s32[1,64]{1,0:T(1,128)} %param.28) | copy-start | bytes 772
  14.3 36.8 %all-to-all-start.1 = ((bf16[16,64,192]{2,1,0:T(8,128)(2,1)}), bf16[16,64,192]{2,1,0:T(8,128)(2,1)S(1)}, u32[]{:S(2)}, u32[]{:S(2)}) async-start(bf16[16,64,192]{2,1,0:T(8,128)(2,1)} %get-tuple-element.212), calls=%async_computation.1 | async-start | bytes 1048576 | tf_op jit(solution)/shard_map/all_to_all | solution.py:171
  22.3 110.1 %all-gather.8.cloned.1.call-start = ((), (), s32[]{:S(2)}) async-start(), calls=%async_computation.5 | async-start | bytes 1327104 | tf_op jit(solution)/shard_map/all_gather | solution.py:185
  51.1 18.4 %all-to-all-start = ((bf16[16,64,192]{2,1,0:T(8,128)(2,1)}), bf16[16,64,192]{2,1,0:T(8,128)(2,1)}, u32[]{:S(2)}, u32[]{:S(2)}) async-start(bf16[16,64,192]{2,1,0:T(8,128)(2,1)} %get-tuple-element.213), calls=%async_computation | async-start | bytes 1048576 | tf_op jit(solution)/shard_map/all_to_all | solution.py:170
  69.5 53.7 %all-to-all-start.2 = ((bf16[16,64,192]{2,1,0:T(8,128)(2,1)}), bf16[16,64,192]{2,1,0:T(8,128)(2,1)}, u32[]{:S(2)}, u32[]{:S(2)}) async-start(bf16[16,64,192]{2,1,0:T(8,128)(2,1)} %get-tuple-element.211), calls=%async_computation.2 | async-start | bytes 1048576 | tf_op jit(solution)/shard_map/all_to_all | solution.py:172
  73.7 119.3 %all-gather.6.cloned.1.call-start = ((), (), s32[]{:S(2)}) async-start(), calls=%async_computation.4 | async-start | bytes 6684672 | tf_op jit(solution)/shard_map/all_gather | solution.py:187
  83.3 3.3 copy-start.1
  89.4 3.4 copy-start
  96.1 3.3 copy-start.1
  102.3 3.4 copy-start
  110.0 3.3 copy-start.1
  116.1 3.4 copy-start
  123.1 3.6 copy-start.10
  126.8 4.1 copy-start.8
  126.8 5.5 %copy-start.9 = (bf16[192]{0:T(256)(128)(2,1)S(1)}, bf16[192]{0:T(256)(128)(2,1)}, u32[]{:S(2)}) copy-start(bf16[192]{0:T(256)(128)(2,1)} %param.32) | copy-start | bytes 1156
  129.9 154.7 %all-gather.12.cloned.1.call-start = ((), (), s32[]{:S(2)}) async-start(), calls=%async_computation.7 | async-start | bytes 3538944 | tf_op jit(solution)/shard_map/all_gather | solution.py:205
  130.6 165.7 %all-gather.10.cloned.1.call-start = ((), (), s32[]{:S(2)}) async-start(), calls=%async_computation.6 | async-start | bytes 6684672 | tf_op jit(solution)/shard_map/all_gather | solution.py:202
  198.0 1.0 copy-start.5
  198.6 40.6 %copy-start.4 = (bf16[384,512]{1,0:T(8,128)(2,1)S(1)}, bf16[384,512]{1,0:T(8,128)(2,1)}, u32[]{:S(2)}) copy-start(bf16[384,512]{1,0:T(8,128)(2,1)} %param.34) | copy-start | bytes 1179652
  238.5 86.7 %all-gather.14.cloned.1.call-start = ((), (), s32[]{:S(2)}) async-start(), calls=%async_computation.8 | async-start | bytes 3538944 | tf_op jit(solution)/shard_map/all_gather | solution.py:214
  239.1 180.9 %reduce-scatter.2.cloned.1.call-start = ((), (), s32[]{:S(2)}) async-start(), calls=%async_computation.9 | async-start | bytes 6684672 | tf_op jit(solution)/shard_map/reduce_scatter | solution.py:217
  239.2 8.4 %collective-permute-start = (bf16[384,512]{1,0:T(8,128)(2,1)S(1)}, bf16[384,512]{1,0:T(8,128)(2,1)S(1)}, u32[]{:S(2)}, u32[]{:S(2)}) collective-permute-start(bf16[384,512]{1,0:T(8,128)(2,1)S(1)} %copy-done.4), channel_id=1, source_target_pairs={{0,16},{16,32},{32,48},{48,64},{64,80},{80,96},{96,112},{112,0},{1... | collective-permute-start | bytes 1179656 | tf_op jit(solution)/shard_map/ppermute | solution.py:32
  247.6 8.4 %collective-permute-start.1 = (bf16[384,512]{1,0:T(8,128)(2,1)S(1)}, bf16[384,512]{1,0:T(8,128)(2,1)S(1)}, u32[]{:S(2)}, u32[]{:S(2)}) collective-permute-start(bf16[384,512]{1,0:T(8,128)(2,1)S(1)} %collective-permute-done), channel_id=1, source_target_pairs={{0,16},{16,32},{32,48},{48,64},{64,80},{80,96},{96,112},{112,0},{1... | collective-permute-start | bytes 1179656 | tf_op jit(solution)/shard_map/ppermute | solution.py:32
  247.6 8.4 %collective-permute-start.4 = (bf16[384,512]{1,0:T(8,128)(2,1)S(1)}, bf16[384,512]{1,0:T(8,128)(2,1)S(1)}, u32[]{:S(2)}, u32[]{:S(2)}) collective-permute-start(bf16[384,512]{1,0:T(8,128)(2,1)S(1)} %copy-done.4), channel_id=1, source_target_pairs={{16,0},{32,16},{48,32},{64,48},{80,64},{96,80},{112,96},{0,112},{1... | collective-permute-start | bytes 1179656 | tf_op jit(solution)/shard_map/ppermute | solution.py:35
  256.0 8.4 %collective-permute-start.2 = (bf16[384,512]{1,0:T(8,128)(2,1)S(1)}, bf16[384,512]{1,0:T(8,128)(2,1)S(1)}, u32[]{:S(2)}, u32[]{:S(2)}) collective-permute-start(bf16[384,512]{1,0:T(8,128)(2,1)S(1)} %collective-permute-done.1), channel_id=1, source_target_pairs={{0,16},{16,32},{32,48},{48,64},{64,80},{80,96},{96,112},{112,0},{1... | collective-permute-start | bytes 1179656 | tf_op jit(solution)/shard_map/ppermute | solution.py:32
  256.0 8.4 %collective-permute-start.5 = (bf16[384,512]{1,0:T(8,128)(2,1)S(1)}, bf16[384,512]{1,0:T(8,128)(2,1)S(1)}, u32[]{:S(2)}, u32[]{:S(2)}) collective-permute-start(bf16[384,512]{1,0:T(8,128)(2,1)S(1)} %collective-permute-done.4), channel_id=1, source_target_pairs={{16,0},{32,16},{48,32},{64,48},{80,64},{96,80},{112,96},{0,112},{1... | collective-permute-start | bytes 1179656 | tf_op jit(solution)/shard_map/ppermute | solution.py:35
  264.4 8.5 %collective-permute-start.3 = (bf16[384,512]{1,0:T(8,128)(2,1)S(1)}, bf16[384,512]{1,0:T(8,128)(2,1)}, u32[]{:S(2)}, u32[]{:S(2)}) collective-permute-start(bf16[384,512]{1,0:T(8,128)(2,1)S(1)} %collective-permute-done.2), channel_id=1, source_target_pairs={{0,16},{16,32},{32,48},{48,64},{64,80},{80,96},{96,112},{112,0},{1... | collective-permute-start | bytes 1179656 | tf_op jit(solution)/shard_map/ppermute | solution.py:32
  264.4 15.0 %collective-permute-start.6 = (bf16[384,512]{1,0:T(8,128)(2,1)S(1)}, bf16[384,512]{1,0:T(8,128)(2,1)S(1)}, u32[]{:S(2)}, u32[]{:S(2)}) collective-permute-start(bf16[384,512]{1,0:T(8,128)(2,1)S(1)} %collective-permute-done.5), channel_id=1, source_target_pairs={{16,0},{32,16},{48,32},{64,48},{80,64},{96,80},{112,96},{0,112},{1... | collective-permute-start | bytes 1179656 | tf_op jit(solution)/shard_map/ppermute | solution.py:35
  338.0 1.0 copy-start.2
  338.0 2.7 copy-start.6
Sparse Core Ops, SparseCore 0:
  24.8 25.2 all-gather.7
  130.0 63.0 all-gather.5
  194.8 27.2 all-gather.11
  238.6 57.6 all-gather.9
  297.9 27.2 all-gather.13
  338.1 81.8 reduce-scatter.1
